TPU v7x, 256 devices: a whole 4x4x8 slice. The times are simulated.
256 devices in a mesh: context: 32 (over x, z), mirror: 2 (over core), tensor: 4 (over y).
Axes of the slice: x: 4, y: 4, z: 8, core: 2. Of those that a mesh axis runs over, the one named last changes fastest.
Arguments:
- hyena_q: bfloat16 [8192, 8192], P(('context', 'mirror'), 'tensor'), may hold values from -57 to 57
- hyena_k: bfloat16 [8192, 8192], P(('context', 'mirror'), 'tensor'), may hold values from -6 to 6
- hyena_v: bfloat16 [8192, 8192], P(('context', 'mirror'), 'tensor'), may hold values from -6 to 6
- filters: bfloat16 [512, 128], P('tensor'), may hold values from -0.5 to 0.5
- norm_gain: float32 [8192], P('tensor'), may hold values from 0.1 to 1.9
- attn_q: bfloat16 [8192, 8192], P(('context', 'mirror'), 'tensor'), may hold values from -35 to 35
- attn_k: bfloat16 [8192, 8192], P(('context', 'mirror'), 'tensor'), may hold values from -5 to 5
- out_grad: bfloat16 [8192, 8192], P(('context', 'mirror'), 'tensor'), may hold values from -20 to 20
- doc_lengths: int32 [4], replicated, may hold values from 1 to 4096, 8192 in all
Outputs:
- attn_out: bfloat16 [8192, 8192], P(('context', 'mirror'), 'tensor')
- grad_attn_q: bfloat16 [8192, 8192], P(('context', 'mirror'), 'tensor')
- grad_attn_k: bfloat16 [8192, 8192], P(('context', 'mirror'), 'tensor')
- grad_hyena_q: bfloat16 [8192, 8192], P(('context', 'mirror'), 'tensor')
- grad_hyena_k: bfloat16 [8192, 8192], P(('context', 'mirror'), 'tensor')
- grad_hyena_v: bfloat16 [8192, 8192], P(('context', 'mirror'), 'tensor')
- grad_filters: float32 [512, 128], P('tensor')
All inputs are finite; a program needn't handle non-finite values.
Results may differ from a plain program's by a relative error of at most 0.0064.
Values may be sent and summed in bfloat16 or wider, within the bound.
No kernel may reach another device: no remote copies, remote signals or barrier semaphores. Data moves between devices by JAX's collectives and lax.ppermute only.
A program may use at most 128 MiB of HBM per device.

v0:
```python
import jax
import jax.numpy as jnp
from jax import lax
from jax.sharding import PartitionSpec as P

HEAD = 128
D = 8192
REACH = 2


def passed_along(block, axis, distance):
    devices = range(lax.axis_size(axis))
    route = [(i - distance, i) for i in devices if i - distance in devices]
    return lax.ppermute(block, axis, route)


def doc_index(doc_lengths, positions):
    doc_ends = jnp.cumsum(doc_lengths, dtype=jnp.int32)
    return jnp.sum(
        (positions[:, None] >= doc_ends[None, :]).astype(jnp.int32), axis=1, dtype=jnp.int32
    )


def banded(band_table, row_count, col_count):
    repeated = jnp.tile(band_table, (1, row_count + 1))[:, : row_count * col_count]
    return repeated.reshape(band_table.shape[0], row_count, col_count)


def attend(queries, key_heads, allowed, score_scale):
    scores = (
        jnp.einsum("thd,uhd->htu", queries, key_heads, preferred_element_type=jnp.float32)
        * score_scale
    )
    row_top = jnp.max(jnp.where(allowed[None], scores, -1e30), axis=2, keepdims=True)
    row_total = jnp.sum(
        jnp.exp(jnp.where(allowed[None], scores - row_top, -1e30)), axis=2, keepdims=True
    )
    row_lse = row_top + jnp.log(row_total)
    return (jnp.where(allowed[None], jnp.exp(scores - row_lse), 0.0), row_lse)


def body(hyena_q, hyena_k, hyena_v, filters, norm_gain, attn_q, attn_k, out_grad, doc_lengths):
    tok_rows, channels = hyena_q.shape
    groups, tap_count = filters.shape
    group_width = channels // groups
    heads_dev = channels // HEAD
    pad_rows = tok_rows + tap_count
    offset = lax.axis_index(("context", "mirror")) * tok_rows
    score_scale = HEAD ** (-0.5)
    window_span = REACH * tok_rows
    own_pos = offset + jnp.arange(tok_rows, dtype=jnp.int32)
    own_doc = doc_index(doc_lengths, own_pos)
    kv_product = (hyena_k.astype(jnp.float32) * hyena_v.astype(jnp.float32)).astype(jnp.bfloat16)
    left_rim = passed_along(kv_product[tok_rows - (tap_count - 1) :], ("context", "mirror"), 1)
    wide_pad = jnp.concatenate(
        [left_rim, kv_product, jnp.zeros((1, channels), jnp.bfloat16)], axis=0
    )
    wide_pos = offset - (tap_count - 1) + jnp.arange(pad_rows, dtype=jnp.int32)
    fwd_mask = own_doc[:, None] == doc_index(doc_lengths, wide_pos)[None, :]
    zeros_tail = jnp.zeros((groups, pad_rows + 1 - tap_count), jnp.bfloat16)
    fwd_table = jnp.concatenate([filters[:, ::-1], zeros_tail], axis=1)
    fwd_band = banded(fwd_table, tok_rows, pad_rows) * fwd_mask[None].astype(jnp.bfloat16)
    wide_groups = wide_pad.reshape(pad_rows, groups, group_width)
    signal = jnp.einsum(
        "gtu,ugc->tgc", fwd_band, wide_groups, preferred_element_type=jnp.float32
    ).reshape(tok_rows, channels)
    hyena_mix = hyena_q.astype(jnp.float32) * signal
    square_sum = lax.psum(jnp.sum(hyena_mix * hyena_mix, axis=1), "tensor")
    inv_rms = lax.rsqrt(square_sum / D + 1e-06)
    values = (hyena_mix * inv_rms[:, None] * norm_gain[None, :]).astype(jnp.bfloat16)
    earlier = []
    for distance in range(1, REACH + 1):
        earlier.append(passed_along((attn_k, values), ("context", "mirror"), distance))
    key_win = jnp.concatenate([piece[0] for piece in earlier[::-1]] + [attn_k], axis=0)
    value_win = jnp.concatenate([piece[1] for piece in earlier[::-1]] + [values], axis=0)
    window = (REACH + 1) * tok_rows
    key_pos = offset - REACH * tok_rows + jnp.arange(window, dtype=jnp.int32)
    key_doc = doc_index(doc_lengths, key_pos)
    allowed = (
        (key_pos[None, :] >= 0)
        & (key_pos[None, :] <= own_pos[:, None])
        & (own_pos[:, None] - key_pos[None, :] <= window_span)
        & (key_doc[None, :] == own_doc[:, None])
    )
    queries = attn_q.reshape(tok_rows, heads_dev, HEAD)
    grad_heads = out_grad.reshape(tok_rows, heads_dev, HEAD)
    key_heads = key_win.reshape(window, heads_dev, HEAD)
    value_heads = value_win.reshape(window, heads_dev, HEAD)
    attn_prob, row_lse = attend(queries, key_heads, allowed, score_scale)
    prob_half = attn_prob.astype(jnp.bfloat16)
    attn_out = (
        jnp.einsum("htu,uhd->thd", prob_half, value_heads, preferred_element_type=jnp.float32)
        .astype(jnp.bfloat16)
        .reshape(tok_rows, channels)
    )
    grad_prob = jnp.einsum(
        "thd,uhd->htu", grad_heads, value_heads, preferred_element_type=jnp.float32
    )
    row_delta = jnp.sum(attn_prob * grad_prob, axis=2, keepdims=True)
    grad_score = (attn_prob * (grad_prob - row_delta) * score_scale).astype(jnp.bfloat16)
    grad_attn_q = (
        jnp.einsum("htu,uhd->thd", grad_score, key_heads, preferred_element_type=jnp.float32)
        .astype(jnp.bfloat16)
        .reshape(tok_rows, channels)
    )
    own_start = REACH * tok_rows
    key_part = jnp.einsum("htu,thd->uhd", grad_score, queries, preferred_element_type=jnp.float32)
    value_part = jnp.einsum(
        "htu,thd->uhd", prob_half, grad_heads, preferred_element_type=jnp.float32
    )
    grad_keys = key_part[own_start:]
    grad_vals = value_part[own_start:]
    for distance in range(1, REACH + 1):
        low_row = (REACH - distance) * tok_rows
        returned = passed_along(
            (key_part[low_row : low_row + tok_rows], value_part[low_row : low_row + tok_rows]),
            ("context", "mirror"),
            -distance,
        )
        grad_keys = grad_keys + returned[0]
        grad_vals = grad_vals + returned[1]
    grad_attn_k = grad_keys.astype(jnp.bfloat16).reshape(tok_rows, channels)
    grad_values = grad_vals.reshape(tok_rows, channels)
    inner_sum = lax.psum(jnp.sum(norm_gain[None, :] * grad_values * hyena_mix, axis=1), "tensor")
    grad_mix = inv_rms[:, None] * (
        norm_gain[None, :] * grad_values - hyena_mix * (inner_sum * inv_rms * inv_rms / D)[:, None]
    )
    grad_hyena_q = (grad_mix * signal).astype(jnp.bfloat16)
    grad_signal = (grad_mix * hyena_q.astype(jnp.float32)).astype(jnp.bfloat16)
    right_rim = passed_along(grad_signal[: tap_count - 1], ("context", "mirror"), -1)
    back_pad = jnp.concatenate(
        [grad_signal, right_rim, jnp.zeros((1, channels), jnp.bfloat16)], axis=0
    )
    back_pos = offset + jnp.arange(pad_rows, dtype=jnp.int32)
    back_mask = own_doc[:, None] == doc_index(doc_lengths, back_pos)[None, :]
    back_table = jnp.concatenate([filters, zeros_tail], axis=1)
    back_band = banded(back_table, tok_rows, pad_rows) * back_mask[None].astype(jnp.bfloat16)
    grad_kv = jnp.einsum(
        "gtu,ugc->tgc",
        back_band,
        back_pad.reshape(pad_rows, groups, group_width),
        preferred_element_type=jnp.float32,
    ).reshape(tok_rows, channels)
    grad_hyena_k = (grad_kv * hyena_v.astype(jnp.float32)).astype(jnp.bfloat16)
    grad_hyena_v = (grad_kv * hyena_k.astype(jnp.float32)).astype(jnp.bfloat16)
    block_count = 4
    block_size = groups // block_count
    mask_float = fwd_mask.astype(jnp.float32)

    def filter_block(pieces):
        grad_block, wide_block = pieces
        correlation = (
            jnp.einsum("tgc,ugc->gtu", grad_block, wide_block, preferred_element_type=jnp.float32)
            * mask_float[None]
        )
        flattened = jnp.pad(
            correlation.reshape(block_size, tok_rows * pad_rows), ((0, 0), (0, tok_rows))
        )
        diagonal = flattened.reshape(block_size, tok_rows, pad_rows + 1)[:, :, :tap_count]
        return jnp.sum(diagonal, axis=1)[:, ::-1]

    grad_blocks = grad_signal.reshape(tok_rows, block_count, block_size, group_width).transpose(
        1, 0, 2, 3
    )
    wide_blocks = wide_groups.reshape(pad_rows, block_count, block_size, group_width).transpose(
        1, 0, 2, 3
    )
    local_filters = lax.map(filter_block, (grad_blocks, wide_blocks)).reshape(groups, tap_count)
    grad_filters = lax.psum(local_filters, ("context", "mirror"))
    return (
        attn_out,
        grad_attn_q,
        grad_attn_k,
        grad_hyena_q,
        grad_hyena_k,
        grad_hyena_v,
        grad_filters,
    )


def solution(mesh):
    return jax.shard_map(
        body,
        mesh=mesh,
        in_specs=(
            P(("context", "mirror"), "tensor"),
            P(("context", "mirror"), "tensor"),
            P(("context", "mirror"), "tensor"),
            P("tensor", None),
            P("tensor"),
            P(("context", "mirror"), "tensor"),
            P(("context", "mirror"), "tensor"),
            P(("context", "mirror"), "tensor"),
            P(),
        ),
        out_specs=(
            P(("context", "mirror"), "tensor"),
            P(("context", "mirror"), "tensor"),
            P(("context", "mirror"), "tensor"),
            P(("context", "mirror"), "tensor"),
            P(("context", "mirror"), "tensor"),
            P(("context", "mirror"), "tensor"),
            P("tensor", None),
        ),
        check_vma=False,
    )
```

profile of v0, /device:TPU:1, one launch (start us, length us, event | category | flops | bytes accessed | tf_op | source)
XLA Modules:
  0.0 418.3 jit_solution(6076285192775258305)
XLA Ops:
  8.6 5.1 %collective-permute-start.4 = (bf16[128,2048]{0,1:T(8,128)(2,1)S(1)}, bf16[128,2048]{0,1:T(8,128)(2,1)}, u32[]{:S(2)}, u32[]{:S(2)}) collective-permute-start(bf16[128,2048]{0,1:T(8,128)(2,1)S(1)} %copy.70), channel_id=1, source_target_pairs={{0,4},{4,8},{8,12},{12,16},{16,20},{20,24},{24,28},{28,32},{32,36}... | collective-permute-start | bytes 1572872 | tf_op jit(solution)/shard_map/ppermute | solution.py:14
  28.5 4.5 %tile.8 = bf16[128,129,257]{0,2,1:T(8,128)(2,1)} broadcast(bf16[128,257]{0,1:T(8,128)(2,1)S(1)} %concatenate.19.clone), dimensions={0,2} | broadcast | bytes 8552960 | tf_op jit(solution)/shard_map/tile | solution.py:25
  33.0 13.2 %tile.9 = bf16[128,33153]{0,1:T(8,128)(2,1)} reshape(bf16[128,129,257]{0,2,1:T(8,128)(2,1)} %tile.8) | data formatting | bytes 16974336 | tf_op jit(solution)/shard_map/tile | solution.py:25
  46.3 7.1 %slice.49 = bf16[128,32768]{0,1:T(8,128)(2,1)} slice(bf16[128,33153]{0,1:T(8,128)(2,1)} %tile.9), slice={[0:128], [0:32768]} | slice | bytes 16777216 | tf_op jit(solution)/shard_map/slice | solution.py:25
  53.3 12.5 %copy.69 = bf16[128,128,256]{2,1,0:T(8,128)(2,1)} copy(bf16[128,128,256]{0,2,1:T(8,128)(2,1)} %bitcast.165) | data formatting | bytes 16777216 | tf_op jit(solution)/shard_map/reshape | solution.py:26
  65.8 4.5 %tile.20 = bf16[128,129,257]{0,2,1:T(8,128)(2,1)} broadcast(bf16[128,257]{0,1:T(8,128)(2,1)S(1)} %concatenate.23.clone), dimensions={0,2} | broadcast | bytes 8552960 | tf_op jit(solution)/shard_map/tile | solution.py:25
  70.3 13.2 %tile.21 = bf16[128,33153]{0,1:T(8,128)(2,1)} reshape(bf16[128,129,257]{0,2,1:T(8,128)(2,1)} %tile.20) | data formatting | bytes 16974336 | tf_op jit(solution)/shard_map/tile | solution.py:25
  83.5 7.1 %slice.57 = bf16[128,32768]{0,1:T(8,128)(2,1)} slice(bf16[128,33153]{0,1:T(8,128)(2,1)} %tile.21), slice={[0:128], [0:32768]} | slice | bytes 16777216 | tf_op jit(solution)/shard_map/slice | solution.py:25
  90.6 12.6 %copy.84 = bf16[128,128,256]{2,1,0:T(8,128)(2,1)} copy(bf16[128,128,256]{0,2,1:T(8,128)(2,1)} %bitcast.166) | data formatting | bytes 16777216 | tf_op jit(solution)/shard_map/reshape | solution.py:26
  116.6 16.7 %collective-permute-done.8 = f32[128,16,128]{0,2,1:T(8,128)S(1)} collective-permute-done((f32[128,16,128]{0,2,1:T(8,128)S(1)}, f32[128,16,128]{0,2,1:T(8,128)S(1)}, u32[]{:S(2)}, u32[]{:S(2)}) %collective-permute-start.8) | collective-permute-done | bytes 1048608 | tf_op jit(solution)/shard_map/ppermute | solution.py:14
  133.3 12.7 %collective-permute-done.7 = f32[128,16,128]{0,2,1:T(8,128)S(1)} collective-permute-done((f32[128,16,128]{0,2,1:T(8,128)S(1)}, f32[128,16,128]{0,2,1:T(8,128)S(1)}, u32[]{:S(2)}, u32[]{:S(2)}) %collective-permute-start.7) | collective-permute-done | bytes 1048608 | tf_op jit(solution)/shard_map/ppermute | solution.py:14
  147.2 8.7 %all-reduce.3 = (f32[128]{0:T(128)S(1)}, f32[128]{0:T(128)S(1)}) all-reduce(f32[128]{0:T(128)S(1)} %get-tuple-element.111, f32[128]{0:T(128)S(1)} %get-tuple-element.110), channel_id=1, replica_groups=mesh['context'=32,'mirror'=2,'tensor'=4] {'tensor'}, use_global_device_ids=true, to_apply=%region_4.5 | all-reduce | flops 256 | bytes 2048 | tf_op jit(solution)/shard_map/psum | solution.py:68
  163.0 5.2 %collective-permute-start.1 = (bf16[128,2048]{0,1:T(8,128)(2,1)}, bf16[128,2048]{0,1:T(8,128)(2,1)}, u32[]{:S(2)}, u32[]{:S(2)}) collective-permute-start(bf16[128,2048]{0,1:T(8,128)(2,1)} %get-tuple-element.134), channel_id=1, source_target_pairs={{0,8},{4,12},{8,16},{12,20},{16,24},{20,28},{24,32},{28,36},{32,40... | collective-permute-start | bytes 1572872 | tf_op jit(solution)/shard_map/ppermute | solution.py:14
  170.1 67.7 %while.13 = (s32[]{:T(128)}, f32[4,32,128]{2,1,0:T(8,128)}, bf16[4,128,32,16]{1,3,2,0:T(8,128)(2,1)}, bf16[4,256,32,16]{1,3,2,0:T(8,128)(2,1)}, s32[256]{0:T(256...) while((s32[]{:T(128)}, f32[4,32,128]{2,1,0:T(8,128)}, bf16[4,128,32,16]{1,3,2,0:T(8,128)(2,1)}, ...), condition=%wide.region_14.15_spmd.clone, body=%wide.region_12.14_spmd.clone.sunk | while | flops 35188736 | bytes 32246372 | solution.py:168
  176.7 8.0 %reshape.319 = f32[32,128,257]{2,1,0:T(8,128)} reshape(f32[32,32896]{1,0:T(8,128)} %pad.33) | data formatting | bytes 8421376 | tf_op jit(solution)/shard_map/while/body/eval_jaxpr/reshape | solution.py:159
  193.6 8.0 %reshape.319 = f32[32,128,257]{2,1,0:T(8,128)} reshape(f32[32,32896]{1,0:T(8,128)} %pad.33) | data formatting | bytes 8421376 | tf_op jit(solution)/shard_map/while/body/eval_jaxpr/reshape | solution.py:159
  210.6 8.0 %reshape.319 = f32[32,128,257]{2,1,0:T(8,128)} reshape(f32[32,32896]{1,0:T(8,128)} %pad.33) | data formatting | bytes 8421376 | tf_op jit(solution)/shard_map/while/body/eval_jaxpr/reshape | solution.py:159
  227.5 8.0 %reshape.319 = f32[32,128,257]{2,1,0:T(8,128)} reshape(f32[32,32896]{1,0:T(8,128)} %pad.33) | data formatting | bytes 8421376 | tf_op jit(solution)/shard_map/while/body/eval_jaxpr/reshape | solution.py:159
  241.4 6.7 %fusion.8 = f32[128,16,128]{2,1,0:T(8,128)} fusion(bf16[256,128,16]{0,2,1:T(8,128)(2,1)S(1)} %bitcast.175, bf16[128,128,256]{2,1,0:T(8,128)(2,1)} %copy.84, bf16[128,256]{1,0:T(8,128)(2,1)S(1)} %get-tuple-element.137), kind=kOutput, calls=%fused_computation.11 | convolution fusion | flops 138412032 | bytes 10551296 | tf_op jit(solution)/shard_map/gtu,ugc->tgc/dot_general | solution.py:138
  253.2 6.6 %convolution_bitcast_fusion.1 = f32[384,16,128]{0,2,1:T(8,128)} fusion(bf16[128,16,128]{0,2,1:T(8,128)(2,1)} %bitcast.177, f32[16,384,128]{2,1,0:T(8,128)} %fusion.72, f32[16,384,128]{2,1,0:T(8,128)S(1)} %get-tuple-element.142, f32[16,128]{1,0:T(8,128)S(1)} %log_add_fusion, pred[128,384]{0,1:T(8,128)(4,1)S(1)} %fusion.54), kind=kOutput, calls=%fused_computation.32 | convolution fusion | flops 209979776 | bytes 10018816 | tf_op jit(solution)/shard_map/htu,thd->uhd/dot_general | solution.py:107
  276.9 6.2 %fusion.44 = bf16[16,128,128]{2,1,0:T(8,128)(2,1)} fusion(bf16[384,16,128]{0,2,1:T(8,128)(2,1)} %bitcast.172, f32[16,384,128]{2,1,0:T(8,128)} %fusion.72, f32[16,384,128]{2,1,0:T(8,128)S(1)} %get-tuple-element.142, f32[16,128]{1,0:T(8,128)S(1)} %log_add_fusion, pred[128,384]{0,1:T(8,128)(4,1)S(1)} %fusion.54), kind=kOutput, calls=%fused_computation.54 | convolution fusion | flops 210241920 | bytes 8445952 | tf_op jit(solution)/shard_map/htu,uhd->thd/dot_general | solution.py:102
  285.2 5.1 %collective-permute-done.6 = f32[128,16,128]{0,2,1:T(8,128)} collective-permute-done((f32[128,16,128]{0,2,1:T(8,128)}, f32[128,16,128]{0,2,1:T(8,128)}, u32[]{:S(2)}, u32[]{:S(2)}) %collective-permute-start.6) | collective-permute-done | bytes 1048608 | tf_op jit(solution)/shard_map/ppermute | solution.py:14
  290.3 11.6 %collective-permute-done.5 = f32[128,16,128]{0,2,1:T(8,128)} collective-permute-done((f32[128,16,128]{0,2,1:T(8,128)}, f32[128,16,128]{0,2,1:T(8,128)}, u32[]{:S(2)}, u32[]{:S(2)}) %collective-permute-start.5) | collective-permute-done | bytes 1048608 | tf_op jit(solution)/shard_map/ppermute | solution.py:14
  304.9 105.0 %all-reduce.6.cloned.1.call-done = f32[128,128]{1,0:T(8,128)} async-done(((f32[128,128]{1,0:T(8,128)}), f32[128,128]{1,0:T(8,128)}) %all-reduce.6.cloned.1.call-update) | async-done | bytes 65552 | tf_op jit(solution)/shard_map/psum | solution.py:169
  (144 shorter events, 107.5 us)
Async XLA Ops:
  7.2 17.6 %copy-start.19 = (bf16[128,128]{1,0:T(8,128)(2,1)S(1)}, bf16[128,128]{1,0:T(8,128)(2,1)}, u32[]{:S(2)}) copy-start(bf16[128,128]{1,0:T(8,128)(2,1)} %param.14) | copy-start | bytes 98308
  7.2 17.9 %copy-start.16 = (bf16[128,2048]{1,0:T(8,128)(2,1)S(1)}, bf16[128,2048]{1,0:T(8,128)(2,1)}, u32[]{:S(2)}) copy-start(bf16[128,2048]{1,0:T(8,128)(2,1)} %param.11) | copy-start | bytes 1572868
  7.2 402.8 %all-reduce.6.cloned.1.call-start = ((), (), s32[]{:S(2)}) async-start(), calls=%async_computation | async-start | bytes 131072 | tf_op jit(solution)/shard_map/psum | solution.py:169
  8.6 17.4 %copy-start.17 = (bf16[128,2048]{1,0:T(8,128)(2,1)S(1)}, bf16[128,2048]{1,0:T(8,128)(2,1)}, u32[]{:S(2)}) copy-start(bf16[128,2048]{1,0:T(8,128)(2,1)} %param.18) | copy-start | bytes 1572868
  8.6 95.0 %collective-permute-start.4 = (bf16[128,2048]{0,1:T(8,128)(2,1)S(1)}, bf16[128,2048]{0,1:T(8,128)(2,1)}, u32[]{:S(2)}, u32[]{:S(2)}) collective-permute-start(bf16[128,2048]{0,1:T(8,128)(2,1)S(1)} %copy.70), channel_id=1, source_target_pairs={{0,4},{4,8},{8,12},{12,16},{16,20},{20,24},{24,28},{28,32},{32,36}... | collective-permute-start | bytes 1572872 | tf_op jit(solution)/shard_map/ppermute | solution.py:14
  13.7 90.0 %collective-permute-start.3 = (bf16[128,2048]{0,1:T(8,128)(2,1)S(1)}, bf16[128,2048]{0,1:T(8,128)(2,1)}, u32[]{:S(2)}, u32[]{:S(2)}) collective-permute-start(bf16[128,2048]{0,1:T(8,128)(2,1)S(1)} %copy.70), channel_id=1, source_target_pairs={{0,8},{4,12},{8,16},{12,20},{16,24},{20,28},{24,32},{28,36},{32,40... | collective-permute-start | bytes 1572872 | tf_op jit(solution)/shard_map/ppermute | solution.py:14
  19.3 9.1 %copy-start.8 = (bf16[128,2048]{0,1:T(8,128)(2,1)}, bf16[128,2048]{0,1:T(8,128)(2,1)S(1)}, u32[]{:S(2)}) copy-start(bf16[128,2048]{0,1:T(8,128)(2,1)S(1)} %copy.67) | copy-start | bytes 1572868
  19.4 7.7 %copy-start.21 = (s32[4]{0:T(128)S(1)}, s32[4]{0:T(128)}, u32[]{:S(2)}) copy-start(s32[4]{0:T(128)} %param.19) | copy-start | bytes 52
  19.4 8.0 %copy-start.18 = (bf16[128,2048]{1,0:T(8,128)(2,1)S(1)}, bf16[128,2048]{1,0:T(8,128)(2,1)}, u32[]{:S(2)}) copy-start(bf16[128,2048]{1,0:T(8,128)(2,1)} %param.16) | copy-start | bytes 1572868
  20.9 12.1 %copy-start.10 = (bf16[128,2048]{0,1:T(8,128)(2,1)}, bf16[128,2048]{0,1:T(8,128)(2,1)S(1)}, u32[]{:S(2)}) copy-start(bf16[128,2048]{0,1:T(8,128)(2,1)S(1)} %copy.66) | copy-start | bytes 1572868
  22.9 89.8 %collective-permute-start = (bf16[127,2048]{0,1:T(8,128)(2,1)}, bf16[127,2048]{0,1:T(8,128)(2,1)}, u32[]{:S(2)}, u32[]{:S(2)}) collective-permute-start(bf16[127,2048]{0,1:T(8,128)(2,1)} %slice.48), channel_id=1, source_target_pairs={{0,4},{4,8},{8,12},{12,16},{16,20},{20,24},{24,28},{28,32},{32,36}... | collective-permute-start | bytes 1560584 | tf_op jit(solution)/shard_map/ppermute | solution.py:14
  105.9 8.3 %slice-start = ((s8[8388608]{0:T(1024)(128)(4,1)}), s8[4194304]{0:T(1024)(128)(4,1)S(1)}, s32[]{:S(2)}) async-start(s8[8388608]{0:T(1024)(128)(4,1)} %bitcast.163), calls=%async_computation.1 | async-start | bytes 8388608
  106.6 7.6 %slice-start.1 = ((s8[8388608]{0:T(1024)(128)(4,1)}), s8[4194304]{0:T(1024)(128)(4,1)S(1)}, s32[]{:S(2)}) async-start(s8[8388608]{0:T(1024)(128)(4,1)} %bitcast.163), calls=%async_computation.2 | async-start | bytes 8388608
  107.7 25.6 %collective-permute-start.8 = (f32[128,16,128]{0,2,1:T(8,128)S(1)}, f32[128,16,128]{0,2,1:T(8,128)S(1)}, u32[]{:S(2)}, u32[]{:S(2)}) collective-permute-start(f32[128,16,128]{0,2,1:T(8,128)S(1)} %get-tuple-element.131), channel_id=1, source_target_pairs={{8,0},{12,4},{16,8},{20,12},{24,16},{28,20},{32,24},{36,28},{40,32... | collective-permute-start | bytes 3145736 | tf_op jit(solution)/shard_map/ppermute | solution.py:14
  109.3 36.7 %collective-permute-start.7 = (f32[128,16,128]{0,2,1:T(8,128)S(1)}, f32[128,16,128]{0,2,1:T(8,128)S(1)}, u32[]{:S(2)}, u32[]{:S(2)}) collective-permute-start(f32[128,16,128]{0,2,1:T(8,128)S(1)} %get-tuple-element.130), channel_id=1, source_target_pairs={{4,0},{8,4},{12,8},{16,12},{20,16},{24,20},{28,24},{32,28},{36,32}... | collective-permute-start | bytes 3145736 | tf_op jit(solution)/shard_map/ppermute | solution.py:14
  116.5 30.0 %copy-start.1 = (f32[128,16,128]{2,1,0:T(8,128)}, f32[128,16,128]{2,1,0:T(8,128)S(1)}, u32[]{:S(2)}) copy-start(f32[128,16,128]{2,1,0:T(8,128)S(1)} %fusion.10) | copy-start | bytes 3145732
  116.5 29.7 %copy-start.5 = (bf16[128,2048]{0,1:T(8,128)(2,1)S(1)}, bf16[128,2048]{0,1:T(8,128)(2,1)}, u32[]{:S(2)}) copy-start(bf16[128,2048]{0,1:T(8,128)(2,1)} %copy.65) | copy-start | bytes 1572868
  116.5 29.6 %copy-start.20 = (f32[2048]{0:T(1024)S(1)}, f32[2048]{0:T(1024)}, u32[]{:S(2)}) copy-start(f32[2048]{0:T(1024)} %param.15) | copy-start | bytes 24580
  159.2 88.9 %collective-permute-start.2 = (bf16[128,2048]{0,1:T(8,128)(2,1)}, bf16[128,2048]{0,1:T(8,128)(2,1)}, u32[]{:S(2)}, u32[]{:S(2)}) collective-permute-start(bf16[128,2048]{0,1:T(8,128)(2,1)} %get-tuple-element.134), channel_id=1, source_target_pairs={{0,4},{4,8},{8,12},{12,16},{16,20},{20,24},{24,28},{28,32},{32,36}... | collective-permute-start | bytes 1572872 | tf_op jit(solution)/shard_map/ppermute | solution.py:14
  163.0 85.1 %collective-permute-start.1 = (bf16[128,2048]{0,1:T(8,128)(2,1)}, bf16[128,2048]{0,1:T(8,128)(2,1)}, u32[]{:S(2)}, u32[]{:S(2)}) collective-permute-start(bf16[128,2048]{0,1:T(8,128)(2,1)} %get-tuple-element.134), channel_id=1, source_target_pairs={{0,8},{4,12},{8,16},{12,20},{16,24},{20,28},{24,32},{28,36},{32,40... | collective-permute-start | bytes 1572872 | tf_op jit(solution)/shard_map/ppermute | solution.py:14
  168.2 71.7 %collective-permute-start.9 = (bf16[127,2048]{0,1:T(8,128)(2,1)}, bf16[127,2048]{0,1:T(8,128)(2,1)}, u32[]{:S(2)}, u32[]{:S(2)}) collective-permute-start(bf16[127,2048]{0,1:T(8,128)(2,1)} %bitcast.150), channel_id=1, source_target_pairs={{4,0},{8,4},{12,8},{16,12},{20,16},{24,20},{28,24},{32,28},{36,32}... | collective-permute-start | bytes 1560584 | tf_op jit(solution)/shard_map/ppermute | solution.py:14
  259.8 6.8 %copy-start.14 = (f32[128,16,128]{2,1,0:T(8,128)S(1)}, f32[128,16,128]{2,1,0:T(8,128)}, u32[]{:S(2)}) copy-start(f32[128,16,128]{2,1,0:T(8,128)} %fusion.8) | copy-start | bytes 3145732
  263.2 27.1 %collective-permute-start.6 = (f32[128,16,128]{0,2,1:T(8,128)}, f32[128,16,128]{0,2,1:T(8,128)}, u32[]{:S(2)}, u32[]{:S(2)}) collective-permute-start(f32[128,16,128]{0,2,1:T(8,128)} %get-tuple-element.129), channel_id=1, source_target_pairs={{8,0},{12,4},{16,8},{20,12},{24,16},{28,20},{32,24},{36,28},{40,32... | collective-permute-start | bytes 3145736 | tf_op jit(solution)/shard_map/ppermute | solution.py:14
  264.5 37.4 %collective-permute-start.5 = (f32[128,16,128]{0,2,1:T(8,128)}, f32[128,16,128]{0,2,1:T(8,128)}, u32[]{:S(2)}, u32[]{:S(2)}) collective-permute-start(f32[128,16,128]{0,2,1:T(8,128)} %get-tuple-element.128), channel_id=1, source_target_pairs={{4,0},{8,4},{12,8},{16,12},{20,16},{24,20},{28,24},{32,28},{36,32}... | collective-permute-start | bytes 3145736 | tf_op jit(solution)/shard_map/ppermute | solution.py:14
  (11 other events, 31.9 us)
Sparse Core Ops, SparseCore 0:
  240.0 169.8 all-reduce.5
where the time goes:
time: 421 us; the launch traced here: 418 us
  local copies, waits for them, and re-layouts  155 us (37%)
  waiting for transfers between devices  151 us (36%)
  matrix products  35.9 us (9%)
  starting transfers between devices  30.6 us (7%)
  other arithmetic  21.9 us (5%)
  between operations  14.5 us (3%)
  blocking collectives  8.7 us (2%)
    psum x1, waiting for transfers between devices, body(): grad_filters = lax.psum(local_filters, ('context', 'mirror'))  105 us
    ppermute x10, waiting for transfers between devices, passed_along(): return lax.ppermute(block, axis, route)  46.1 us
    another operation x4, local copies, waits for them, and re-layouts, banded(): jnp.tile(band_table, (1, row_count + 1))[:, :row_count * col_count]  35.4 us
    reshape x4, local copies, waits for them, and re-layouts, filter_block(): flattened.reshape(block_size, tok_rows, pad_rows + 1)[:, :, :tap_count]  31.8 us
    ppermute x10, starting transfers between devices, passed_along(): return lax.ppermute(block, axis, route)  30.6 us
    reshape x2, local copies, waits for them, and re-layouts, banded(): return repeated.reshape(band_table.shape[0], row_count, col_count)  25 us
    unnamed x61, local copies, waits for them, and re-layouts  20.7 us
    slice x2, local copies, waits for them, and re-layouts, banded(): jnp.tile(band_table, (1, row_count + 1))[:, :row_count * col_count]  14.1 us
  transfers between devices with their start and end apart: 11, of which 5 were waited for; matrix products, arithmetic and copies ran while one was open for 49% of the time, Pallas kernels for 0%

commit v1 on v0

--- a/solution.py
+++ b/solution.py
@@ -166,7 +166,7 @@
         1, 0, 2, 3
     )
     local_filters = lax.map(filter_block, (grad_blocks, wide_blocks)).reshape(groups, tap_count)
-    grad_filters = lax.psum(local_filters, ("context", "mirror"))
+    grad_filters = lax.psum(lax.psum(local_filters, "context"), "mirror")
     return (
         attn_out,
         grad_attn_q,

time: 421 us -> 406 us (0.964)
  waiting for transfers between devices: 151 us -> 131 us
  starting transfers between devices: 30.6 us -> 35.3 us
    psum x1 -> x2, waiting for transfers between devices: 105 us -> 89.6 us  [body(): grad_filters = lax.psum(lax.psum(local_filters, 'context'), 'mirror')]
    ppermute x10, waiting for transfers between devices: 46.1 us -> 41.3 us  [passed_along(): return lax.ppermute(block, axis, route)]
    ppermute x10, starting transfers between devices: 30.6 us -> 35.3 us  [passed_along(): return lax.ppermute(block, axis, route)]
    unnamed x61 -> x63, local copies, waits for them, and re-layouts: 20.7 us -> 20.8 us
  transfers between devices with their start and end apart: 11 -> 12, of which waited for: 5 -> 4; matrix products, arithmetic and copies ran while one was open for 49% -> 51% of each run, Pallas kernels for 0% -> 0%
where the time goes in v1:
time: 406 us; the launch traced here: 403 us
  local copies, waits for them, and re-layouts  156 us (38%)
  waiting for transfers between devices  131 us (32%)
  matrix products  35.8 us (9%)
  starting transfers between devices  35.3 us (9%)
  other arithmetic  21.7 us (5%)
  between operations  14.6 us (4%)
  blocking collectives  8.69 us (2%)
    psum x2, waiting for transfers between devices, body(): grad_filters = lax.psum(lax.psum(local_filters, 'context'), 'mirror')  89.6 us
    ppermute x10, waiting for transfers between devices, passed_along(): return lax.ppermute(block, axis, route)  41.3 us
    another operation x4, local copies, waits for them, and re-layouts, banded(): jnp.tile(band_table, (1, row_count + 1))[:, :row_count * col_count]  35.3 us
    ppermute x10, starting transfers between devices, passed_along(): return lax.ppermute(block, axis, route)  35.3 us
    reshape x4, local copies, waits for them, and re-layouts, filter_block(): flattened.reshape(block_size, tok_rows, pad_rows + 1)[:, :, :tap_count]  31.9 us
    reshape x2, local copies, waits for them, and re-layouts, banded(): return repeated.reshape(band_table.shape[0], row_count, col_count)  25.3 us
    unnamed x63, local copies, waits for them, and re-layouts  20.8 us
    slice x2, local copies, waits for them, and re-layouts, banded(): jnp.tile(band_table, (1, row_count + 1))[:, :row_count * col_count]  14.2 us
  transfers between devices with their start and end apart: 12, of which 4 were waited for; matrix products, arithmetic and copies ran while one was open for 51% of the time, Pallas kernels for 0%

profile of v1, /device:TPU:1, one launch (start us, length us, event | category | flops | bytes accessed | tf_op | source)
XLA Modules:
  0.0 403.1 jit_solution(4384621251170008782)
XLA Ops:
  8.6 5.1 %collective-permute-start.4 = (bf16[128,2048]{0,1:T(8,128)(2,1)S(1)}, bf16[128,2048]{0,1:T(8,128)(2,1)}, u32[]{:S(2)}, u32[]{:S(2)}) collective-permute-start(bf16[128,2048]{0,1:T(8,128)(2,1)S(1)} %copy.70), channel_id=1, source_target_pairs={{0,4},{4,8},{8,12},{12,16},{16,20},{20,24},{24,28},{28,32},{32,36}... | collective-permute-start | bytes 1572872 | tf_op jit(solution)/shard_map/ppermute | solution.py:14
  28.4 4.4 %tile.8 = bf16[128,129,257]{0,2,1:T(8,128)(2,1)} broadcast(bf16[128,257]{0,1:T(8,128)(2,1)S(1)} %concatenate.19.clone), dimensions={0,2} | broadcast | bytes 8552960 | tf_op jit(solution)/shard_map/tile | solution.py:25
  32.9 13.2 %tile.9 = bf16[128,33153]{0,1:T(8,128)(2,1)} reshape(bf16[128,129,257]{0,2,1:T(8,128)(2,1)} %tile.8) | data formatting | bytes 16974336 | tf_op jit(solution)/shard_map/tile | solution.py:25
  46.1 7.0 %slice.49 = bf16[128,32768]{0,1:T(8,128)(2,1)} slice(bf16[128,33153]{0,1:T(8,128)(2,1)} %tile.9), slice={[0:128], [0:32768]} | slice | bytes 16777216 | tf_op jit(solution)/shard_map/slice | solution.py:25
  53.1 12.4 %copy.69 = bf16[128,128,256]{2,1,0:T(8,128)(2,1)} copy(bf16[128,128,256]{0,2,1:T(8,128)(2,1)} %bitcast.165) | data formatting | bytes 16777216 | tf_op jit(solution)/shard_map/reshape | solution.py:26
  78.8 16.9 %collective-permute-done.8 = f32[128,16,128]{0,2,1:T(8,128)S(1)} collective-permute-done((f32[128,16,128]{0,2,1:T(8,128)S(1)}, f32[128,16,128]{0,2,1:T(8,128)S(1)}, u32[]{:S(2)}, u32[]{:S(2)}) %collective-permute-start.8) | collective-permute-done | bytes 1048608 | tf_op jit(solution)/shard_map/ppermute | solution.py:14
  95.7 12.7 %collective-permute-done.7 = f32[128,16,128]{0,2,1:T(8,128)S(1)} collective-permute-done((f32[128,16,128]{0,2,1:T(8,128)S(1)}, f32[128,16,128]{0,2,1:T(8,128)S(1)}, u32[]{:S(2)}, u32[]{:S(2)}) %collective-permute-start.7) | collective-permute-done | bytes 1048608 | tf_op jit(solution)/shard_map/ppermute | solution.py:14
  109.6 8.7 %all-reduce.3 = (f32[128]{0:T(128)S(1)}, f32[128]{0:T(128)S(1)}) all-reduce(f32[128]{0:T(128)S(1)} %get-tuple-element.111, f32[128]{0:T(128)S(1)} %get-tuple-element.110), channel_id=1, replica_groups=mesh['context'=32,'mirror'=2,'tensor'=4] {'tensor'}, use_global_device_ids=true, to_apply=%region_4.5 | all-reduce | flops 256 | bytes 2048 | tf_op jit(solution)/shard_map/psum | solution.py:68
  123.8 68.1 %while.13 = (s32[]{:T(128)}, f32[4,32,128]{2,1,0:T(8,128)}, bf16[4,128,32,16]{1,3,2,0:T(8,128)(2,1)}, bf16[4,256,32,16]{1,3,2,0:T(8,128)(2,1)}, s32[256]{0:T(256...) while((s32[]{:T(128)}, f32[4,32,128]{2,1,0:T(8,128)}, bf16[4,128,32,16]{1,3,2,0:T(8,128)(2,1)}, ...), condition=%wide.region_14.15_spmd.clone, body=%wide.region_12.14_spmd.clone.sunk | while | flops 35188736 | bytes 32246372 | solution.py:168
  130.5 8.0 %reshape.319 = f32[32,128,257]{2,1,0:T(8,128)} reshape(f32[32,32896]{1,0:T(8,128)} %pad.33) | data formatting | bytes 8421376 | tf_op jit(solution)/shard_map/while/body/eval_jaxpr/reshape | solution.py:159
  147.5 8.0 %reshape.319 = f32[32,128,257]{2,1,0:T(8,128)} reshape(f32[32,32896]{1,0:T(8,128)} %pad.33) | data formatting | bytes 8421376 | tf_op jit(solution)/shard_map/while/body/eval_jaxpr/reshape | solution.py:159
  164.5 8.0 %reshape.319 = f32[32,128,257]{2,1,0:T(8,128)} reshape(f32[32,32896]{1,0:T(8,128)} %pad.33) | data formatting | bytes 8421376 | tf_op jit(solution)/shard_map/while/body/eval_jaxpr/reshape | solution.py:159
  181.5 8.0 %reshape.319 = f32[32,128,257]{2,1,0:T(8,128)} reshape(f32[32,32896]{1,0:T(8,128)} %pad.33) | data formatting | bytes 8421376 | tf_op jit(solution)/shard_map/while/body/eval_jaxpr/reshape | solution.py:159
  192.1 4.4 %tile.20 = bf16[128,129,257]{0,2,1:T(8,128)(2,1)} broadcast(bf16[128,257]{0,1:T(8,128)(2,1)S(1)} %concatenate.23.clone), dimensions={0,2} | broadcast | bytes 8552960 | tf_op jit(solution)/shard_map/tile | solution.py:25
  196.6 13.2 %tile.21 = bf16[128,33153]{0,1:T(8,128)(2,1)} reshape(bf16[128,129,257]{0,2,1:T(8,128)(2,1)} %tile.20) | data formatting | bytes 16974336 | tf_op jit(solution)/shard_map/tile | solution.py:25
  209.8 7.1 %slice.57 = bf16[128,32768]{0,1:T(8,128)(2,1)} slice(bf16[128,33153]{0,1:T(8,128)(2,1)} %tile.21), slice={[0:128], [0:32768]} | slice | bytes 16777216 | tf_op jit(solution)/shard_map/slice | solution.py:25
  216.9 12.9 %copy.84 = bf16[128,128,256]{2,1,0:T(8,128)(2,1)} copy(bf16[128,128,256]{0,2,1:T(8,128)(2,1)} %bitcast.166) | data formatting | bytes 16777216 | tf_op jit(solution)/shard_map/reshape | solution.py:26
  233.5 5.2 %collective-permute-start.1 = (bf16[128,2048]{0,1:T(8,128)(2,1)}, bf16[128,2048]{0,1:T(8,128)(2,1)}, u32[]{:S(2)}, u32[]{:S(2)}) collective-permute-start(bf16[128,2048]{0,1:T(8,128)(2,1)} %get-tuple-element.134), channel_id=1, source_target_pairs={{0,8},{4,12},{8,16},{12,20},{16,24},{20,28},{24,32},{28,36},{32,40... | collective-permute-start | bytes 1572872 | tf_op jit(solution)/shard_map/ppermute | solution.py:14
  240.7 89.6 %all-reduce.7.cloned.1.call-done = f32[128,128]{1,0:T(8,128)} async-done(((f32[128,128]{1,0:T(8,128)}), f32[128,128]{1,0:T(8,128)}) %all-reduce.7.cloned.1.call-update) | async-done | bytes 65552 | tf_op jit(solution)/shard_map/psum | solution.py:169
  331.8 6.7 %fusion.8 = f32[128,16,128]{2,1,0:T(8,128)} fusion(bf16[256,128,16]{0,2,1:T(8,128)(2,1)S(1)} %bitcast.175, bf16[128,128,256]{2,1,0:T(8,128)(2,1)} %copy.84, bf16[128,256]{1,0:T(8,128)(2,1)S(1)} %get-tuple-element.137), kind=kOutput, calls=%fused_computation.11 | convolution fusion | flops 138412032 | bytes 10551296 | tf_op jit(solution)/shard_map/gtu,ugc->tgc/dot_general | solution.py:138
  343.6 6.6 %convolution_bitcast_fusion.1 = f32[384,16,128]{0,2,1:T(8,128)} fusion(bf16[128,16,128]{0,2,1:T(8,128)(2,1)} %bitcast.177, f32[16,384,128]{2,1,0:T(8,128)} %fusion.72, f32[16,384,128]{2,1,0:T(8,128)S(1)} %get-tuple-element.142, f32[16,128]{1,0:T(8,128)S(1)} %log_add_fusion, pred[128,384]{0,1:T(8,128)(4,1)S(1)} %fusion.54), kind=kOutput, calls=%fused_computation.32 | convolution fusion | flops 209979776 | bytes 10018816 | tf_op jit(solution)/shard_map/htu,thd->uhd/dot_general | solution.py:107
  354.7 6.9 %collective-permute-start.5 = (f32[128,16,128]{0,2,1:T(8,128)}, f32[128,16,128]{0,2,1:T(8,128)}, u32[]{:S(2)}, u32[]{:S(2)}) collective-permute-start(f32[128,16,128]{0,2,1:T(8,128)} %get-tuple-element.128), channel_id=1, source_target_pairs={{4,0},{8,4},{12,8},{16,12},{20,16},{24,20},{28,24},{32,28},{36,32}... | collective-permute-start | bytes 3145736 | tf_op jit(solution)/shard_map/ppermute | solution.py:14
  371.9 6.1 %fusion.44 = bf16[16,128,128]{2,1,0:T(8,128)(2,1)} fusion(bf16[384,16,128]{0,2,1:T(8,128)(2,1)} %bitcast.172, f32[16,384,128]{2,1,0:T(8,128)} %fusion.72, f32[16,384,128]{2,1,0:T(8,128)S(1)} %get-tuple-element.142, f32[16,128]{1,0:T(8,128)S(1)} %log_add_fusion, pred[128,384]{0,1:T(8,128)(4,1)S(1)} %fusion.54), kind=kOutput, calls=%fused_computation.54 | convolution fusion | flops 210241920 | bytes 8445952 | tf_op jit(solution)/shard_map/htu,uhd->thd/dot_general | solution.py:102
  380.1 11.7 %collective-permute-done.5 = f32[128,16,128]{0,2,1:T(8,128)} collective-permute-done((f32[128,16,128]{0,2,1:T(8,128)}, f32[128,16,128]{0,2,1:T(8,128)}, u32[]{:S(2)}, u32[]{:S(2)}) %collective-permute-start.5) | collective-permute-done | bytes 1048608 | tf_op jit(solution)/shard_map/ppermute | solution.py:14
  (149 shorter events, 105.6 us)
Async XLA Ops:
  7.2 17.6 %copy-start.17 = (bf16[128,2048]{1,0:T(8,128)(2,1)S(1)}, bf16[128,2048]{1,0:T(8,128)(2,1)}, u32[]{:S(2)}) copy-start(bf16[128,2048]{1,0:T(8,128)(2,1)} %param.11) | copy-start | bytes 1572868
  7.2 323.1 %all-reduce.7.cloned.1.call-start = ((), (), s32[]{:S(2)}) async-start(), calls=%async_computation | async-start | bytes 131072 | tf_op jit(solution)/shard_map/psum | solution.py:169
  8.6 17.2 %copy-start.18 = (bf16[128,2048]{1,0:T(8,128)(2,1)S(1)}, bf16[128,2048]{1,0:T(8,128)(2,1)}, u32[]{:S(2)}) copy-start(bf16[128,2048]{1,0:T(8,128)(2,1)} %param.18) | copy-start | bytes 1572868
  8.6 57.4 %collective-permute-start.4 = (bf16[128,2048]{0,1:T(8,128)(2,1)S(1)}, bf16[128,2048]{0,1:T(8,128)(2,1)}, u32[]{:S(2)}, u32[]{:S(2)}) collective-permute-start(bf16[128,2048]{0,1:T(8,128)(2,1)S(1)} %copy.70), channel_id=1, source_target_pairs={{0,4},{4,8},{8,12},{12,16},{16,20},{20,24},{24,28},{28,32},{32,36}... | collective-permute-start | bytes 1572872 | tf_op jit(solution)/shard_map/ppermute | solution.py:14
  13.7 52.4 %collective-permute-start.3 = (bf16[128,2048]{0,1:T(8,128)(2,1)S(1)}, bf16[128,2048]{0,1:T(8,128)(2,1)}, u32[]{:S(2)}, u32[]{:S(2)}) collective-permute-start(bf16[128,2048]{0,1:T(8,128)(2,1)S(1)} %copy.70), channel_id=1, source_target_pairs={{0,8},{4,12},{8,16},{12,20},{16,24},{20,28},{24,32},{28,36},{32,40... | collective-permute-start | bytes 1572872 | tf_op jit(solution)/shard_map/ppermute | solution.py:14
  19.3 8.8 %copy-start.8 = (bf16[128,2048]{0,1:T(8,128)(2,1)}, bf16[128,2048]{0,1:T(8,128)(2,1)S(1)}, u32[]{:S(2)}) copy-start(bf16[128,2048]{0,1:T(8,128)(2,1)S(1)} %copy.67) | copy-start | bytes 1572868
  19.4 7.8 %copy-start.19 = (bf16[128,2048]{1,0:T(8,128)(2,1)S(1)}, bf16[128,2048]{1,0:T(8,128)(2,1)}, u32[]{:S(2)}) copy-start(bf16[128,2048]{1,0:T(8,128)(2,1)} %param.16) | copy-start | bytes 1572868
  20.9 12.0 %copy-start.10 = (bf16[128,2048]{0,1:T(8,128)(2,1)}, bf16[128,2048]{0,1:T(8,128)(2,1)S(1)}, u32[]{:S(2)}) copy-start(bf16[128,2048]{0,1:T(8,128)(2,1)S(1)} %copy.66) | copy-start | bytes 1572868
  22.9 52.0 %collective-permute-start = (bf16[127,2048]{0,1:T(8,128)(2,1)}, bf16[127,2048]{0,1:T(8,128)(2,1)}, u32[]{:S(2)}, u32[]{:S(2)}) collective-permute-start(bf16[127,2048]{0,1:T(8,128)(2,1)} %slice.48), channel_id=1, source_target_pairs={{0,4},{4,8},{8,12},{12,16},{16,20},{20,24},{24,28},{28,32},{32,36}... | collective-permute-start | bytes 1560584 | tf_op jit(solution)/shard_map/ppermute | solution.py:14
  68.3 8.1 %slice-start = ((s8[8388608]{0:T(1024)(128)(4,1)}), s8[4194304]{0:T(1024)(128)(4,1)S(1)}, s32[]{:S(2)}) async-start(s8[8388608]{0:T(1024)(128)(4,1)} %bitcast.163), calls=%async_computation.2 | async-start | bytes 8388608
  70.1 25.6 %collective-permute-start.8 = (f32[128,16,128]{0,2,1:T(8,128)S(1)}, f32[128,16,128]{0,2,1:T(8,128)S(1)}, u32[]{:S(2)}, u32[]{:S(2)}) collective-permute-start(f32[128,16,128]{0,2,1:T(8,128)S(1)} %get-tuple-element.131), channel_id=1, source_target_pairs={{8,0},{12,4},{16,8},{20,12},{24,16},{28,20},{32,24},{36,28},{40,32... | collective-permute-start | bytes 3145736 | tf_op jit(solution)/shard_map/ppermute | solution.py:14
  71.7 36.7 %collective-permute-start.7 = (f32[128,16,128]{0,2,1:T(8,128)S(1)}, f32[128,16,128]{0,2,1:T(8,128)S(1)}, u32[]{:S(2)}, u32[]{:S(2)}) collective-permute-start(f32[128,16,128]{0,2,1:T(8,128)S(1)} %get-tuple-element.130), channel_id=1, source_target_pairs={{4,0},{8,4},{12,8},{16,12},{20,16},{24,20},{28,24},{32,28},{36,32}... | collective-permute-start | bytes 3145736 | tf_op jit(solution)/shard_map/ppermute | solution.py:14
  78.7 30.2 %copy-start.1 = (f32[128,16,128]{2,1,0:T(8,128)}, f32[128,16,128]{2,1,0:T(8,128)S(1)}, u32[]{:S(2)}) copy-start(f32[128,16,128]{2,1,0:T(8,128)S(1)} %fusion.10) | copy-start | bytes 3145732
  78.7 29.8 %copy-start.5 = (bf16[128,2048]{0,1:T(8,128)(2,1)S(1)}, bf16[128,2048]{0,1:T(8,128)(2,1)}, u32[]{:S(2)}) copy-start(bf16[128,2048]{0,1:T(8,128)(2,1)} %copy.65) | copy-start | bytes 1572868
  78.8 29.8 %copy-start.21 = (f32[2048]{0:T(1024)S(1)}, f32[2048]{0:T(1024)}, u32[]{:S(2)}) copy-start(f32[2048]{0:T(1024)} %param.15) | copy-start | bytes 24580
  121.7 208.7 %collective-permute-start.9 = (bf16[127,2048]{0,1:T(8,128)(2,1)}, bf16[127,2048]{0,1:T(8,128)(2,1)}, u32[]{:S(2)}, u32[]{:S(2)}) collective-permute-start(bf16[127,2048]{0,1:T(8,128)(2,1)} %bitcast.150), channel_id=1, source_target_pairs={{4,0},{8,4},{12,8},{16,12},{20,16},{24,20},{28,24},{32,28},{36,32}... | collective-permute-start | bytes 1560584 | tf_op jit(solution)/shard_map/ppermute | solution.py:14
  191.9 202.9 %all-reduce.9.cloned.1.call-start = ((), (), s32[]{:S(2)}) async-start(), calls=%async_computation.1 | async-start | bytes 131072 | tf_op jit(solution)/shard_map/psum | solution.py:169
  229.7 108.8 %collective-permute-start.2 = (bf16[128,2048]{0,1:T(8,128)(2,1)}, bf16[128,2048]{0,1:T(8,128)(2,1)}, u32[]{:S(2)}, u32[]{:S(2)}) collective-permute-start(bf16[128,2048]{0,1:T(8,128)(2,1)} %get-tuple-element.134), channel_id=1, source_target_pairs={{0,4},{4,8},{8,12},{12,16},{16,20},{20,24},{24,28},{28,32},{32,36}... | collective-permute-start | bytes 1572872 | tf_op jit(solution)/shard_map/ppermute | solution.py:14
  233.5 105.1 %collective-permute-start.1 = (bf16[128,2048]{0,1:T(8,128)(2,1)}, bf16[128,2048]{0,1:T(8,128)(2,1)}, u32[]{:S(2)}, u32[]{:S(2)}) collective-permute-start(bf16[128,2048]{0,1:T(8,128)(2,1)} %get-tuple-element.134), channel_id=1, source_target_pairs={{0,8},{4,12},{8,16},{12,20},{16,24},{20,28},{24,32},{28,36},{32,40... | collective-permute-start | bytes 1572872 | tf_op jit(solution)/shard_map/ppermute | solution.py:14
  350.2 11.4 %copy-start.9 = (bf16[128,2048]{0,1:T(8,128)(2,1)S(1)}, bf16[128,2048]{0,1:T(8,128)(2,1)}, u32[]{:S(2)}) copy-start(bf16[128,2048]{0,1:T(8,128)(2,1)} %copy-done.8) | copy-start | bytes 1572868
  350.2 11.4 %copy-start.11 = (bf16[128,2048]{0,1:T(8,128)(2,1)S(1)}, bf16[128,2048]{0,1:T(8,128)(2,1)}, u32[]{:S(2)}) copy-start(bf16[128,2048]{0,1:T(8,128)(2,1)} %copy-done.10) | copy-start | bytes 1572868
  350.2 11.4 %copy-start.14 = (f32[128,16,128]{2,1,0:T(8,128)S(1)}, f32[128,16,128]{2,1,0:T(8,128)}, u32[]{:S(2)}) copy-start(f32[128,16,128]{2,1,0:T(8,128)} %fusion.8) | copy-start | bytes 3145732
  353.4 26.6 %collective-permute-start.6 = (f32[128,16,128]{0,2,1:T(8,128)}, f32[128,16,128]{0,2,1:T(8,128)}, u32[]{:S(2)}, u32[]{:S(2)}) collective-permute-start(f32[128,16,128]{0,2,1:T(8,128)} %get-tuple-element.129), channel_id=1, source_target_pairs={{8,0},{12,4},{16,8},{20,12},{24,16},{28,20},{32,24},{36,28},{40,32... | collective-permute-start | bytes 3145736 | tf_op jit(solution)/shard_map/ppermute | solution.py:14
  354.7 37.0 %collective-permute-start.5 = (f32[128,16,128]{0,2,1:T(8,128)}, f32[128,16,128]{0,2,1:T(8,128)}, u32[]{:S(2)}, u32[]{:S(2)}) collective-permute-start(f32[128,16,128]{0,2,1:T(8,128)} %get-tuple-element.128), channel_id=1, source_target_pairs={{4,0},{8,4},{12,8},{16,12},{20,16},{24,20},{28,24},{32,28},{36,32}... | collective-permute-start | bytes 3145736 | tf_op jit(solution)/shard_map/ppermute | solution.py:14
  (13 other events, 46.9 us)
Sparse Core Ops, SparseCore 0:
  192.1 138.2 all-reduce.6
  332.9 31.7 all-reduce.8
